TPU v7x, 32 devices: a whole 2x2x4 slice. The times are simulated.
32 devices in a mesh: groups: 2 (over y), fsdp: 4 (over x, core), tensor: 4 (over z).
Axes of the slice: x: 2, y: 2, z: 4, core: 2. Of those that a mesh axis runs over, the one named last changes fastest.
Arguments:
- tokens: bfloat16 [1024, 8192], P(('groups', 'fsdp')), parts along dimension 0, may hold values from -64 to 64
- gate_weight: bfloat16 [8192, 14336], P('fsdp', 'tensor'), may hold values from -0.0625 to 0.0625
- up_weight: bfloat16 [8192, 14336], P('fsdp', 'tensor'), may hold values from -0.0625 to 0.0625
- down_weight: bfloat16 [14336, 8192], P('tensor', 'fsdp'), may hold values from -0.046875 to 0.046875
- right_factor: bfloat16 [64, 128, 128], P('fsdp', 'tensor'), may hold values from -0.5 to 0.5
- left_factor: bfloat16 [128, 64, 64], P('fsdp', 'tensor'), may hold values from -0.75 to 0.75
Outputs:
- grad_right: float32 [128, 128, 128], P(('groups', 'fsdp'), 'tensor'), parts along dimension 0
- grad_left: float32 [256, 64, 64], P(('groups', 'fsdp'), 'tensor'), parts along dimension 0
There are 2 independent parts, one for each index of `groups`. A program takes and returns all parts, laid end to end along the dimension named above; an argument that names none is the same for every part. Nothing has to cross between parts.
All inputs are finite; a program needn't handle non-finite values.
Results may differ from a plain program's by a relative error of at most 0.0055.
Values may be sent and summed in bfloat16 or wider, within the bound.
A program may use at most 128 MiB of HBM per device.

v0:
```python
import math
import jax
import jax.numpy as jnp
from jax import lax
from jax.sharding import PartitionSpec as P


def body(tokens, gate_weight, up_weight, down_weight, right_factor, left_factor):
    fsdp_count = lax.axis_size("fsdp")
    tensor_count = lax.axis_size("tensor")
    tok_local = tokens.shape[0]
    group_rows = tok_local * fsdp_count
    share_rows = group_rows // tensor_count
    hid_local = gate_weight.shape[1]
    spread = lax.all_to_all(tokens, "fsdp", split_axis=1, concat_axis=0, tiled=True)
    student_in = lax.dynamic_slice_in_dim(
        spread, lax.axis_index("tensor") * share_rows, share_rows, 0
    )
    gate_part = jnp.dot(spread, gate_weight, preferred_element_type=jnp.float32)
    up_part = jnp.dot(spread, up_weight, preferred_element_type=jnp.float32)
    partial_value = jnp.concatenate([gate_part, up_part], axis=1)
    summed = lax.psum(partial_value.astype(jnp.bfloat16), "fsdp").astype(jnp.float32)
    hidden = (jax.nn.silu(summed[:, :hid_local]) * summed[:, hid_local:]).astype(jnp.bfloat16)
    target = lax.psum_scatter(
        jnp.dot(hidden, down_weight, preferred_element_type=jnp.float32).astype(jnp.bfloat16),
        "tensor",
        scatter_dimension=0,
        tiled=True,
    ).astype(jnp.float32)
    right_full, left_full = (
        lax.all_gather(right_factor, "tensor", axis=1, tiled=True),
        lax.all_gather(left_factor, "tensor", axis=1, tiled=True),
    )
    blocks_local = right_full.shape[0]
    block_size = right_full.shape[2]
    block_input = student_in.reshape(share_rows, blocks_local, block_size)
    mixed = jnp.einsum(
        "nij,ikj->nik", block_input, right_full, preferred_element_type=jnp.float32
    ).astype(jnp.bfloat16)
    routed = lax.all_to_all(mixed, "fsdp", split_axis=2, concat_axis=1, tiled=True)
    student = jnp.einsum("nij,jki->njk", routed, left_full, preferred_element_type=jnp.float32)
    inv_root = 1.0 / math.sqrt(group_rows)
    out_grad = (student - target.reshape(student.shape)) * inv_root
    grad_left = jnp.einsum("njk,nij->jki", out_grad, routed.astype(jnp.float32))
    mixed_grad = jnp.einsum("njk,jki->nij", out_grad, left_full.astype(jnp.float32)).astype(
        jnp.bfloat16
    )
    returned = lax.all_to_all(mixed_grad, "fsdp", split_axis=1, concat_axis=2, tiled=True)
    grad_right = jnp.einsum(
        "nik,nij->ikj", returned.astype(jnp.float32), block_input.astype(jnp.float32)
    )
    grad_right, grad_left = (
        lax.psum_scatter(grad_right, "tensor", scatter_dimension=1, tiled=True),
        lax.psum_scatter(grad_left, "tensor", scatter_dimension=1, tiled=True),
    )
    return (grad_right, grad_left)


def solution(mesh):
    return jax.shard_map(
        body,
        mesh=mesh,
        in_specs=(
            P(("groups", "fsdp"), None),
            P("fsdp", "tensor"),
            P("fsdp", "tensor"),
            P("tensor", "fsdp"),
            P("fsdp", "tensor", None),
            P("fsdp", "tensor", None),
        ),
        out_specs=(P(("groups", "fsdp"), "tensor", None), P(("groups", "fsdp"), "tensor", None)),
        check_vma=False,
    )
```

profile of v0, /device:TPU:0, one launch (start us, length us, event | category | flops | bytes accessed | tf_op | source)
XLA Modules:
  0.0 363.5 jit_solution(13968210217118573609)
XLA Ops:
  7.2 0.0 all-reduce.2.cloned.1.call-start
  7.2 4.1 %copy.27 = bf16[128,8192]{0,1:T(8,128)(2,1)} copy(bf16[128,8192]{1,0:T(8,128)(2,1)} %param.6) | data formatting | bytes 4194304 | tf_op args[0]
  11.3 29.9 %all_to_all.55 = bf16[128,4,2048]{0,2,1:T(8,128)(2,1)S(1)} all-to-all(bf16[128,4,2048]{0,2,1:T(8,128)(2,1)} %bitcast.39), channel_id=1, replica_groups=mesh['groups'=2,'fsdp'=4,'tensor'=4] {'fsdp'}, dimensions={1} | all-to-all | bytes 4194304 | tf_op jit(solution)/shard_map/all_to_all | solution.py:15
  41.2 2.6 copy.28
  43.8 0.0 copy-start
  43.8 13.7 %convolution_convert_fusion = bf16[512,3584]{1,0:T(8,128)(2,1)S(1)} fusion(bf16[512,2048]{1,0:T(8,128)(2,1)} %bitcast.45, bf16[2048,3584]{1,0:T(8,128)(2,1)} %param.8), kind=kOutput, calls=%fused_computation.3 | convolution fusion | flops 7518027776 | bytes 20447232 | tf_op jit(solution)/shard_map/dot_general | solution.py:20
  57.5 0.0 copy-done
  57.5 12.4 %convolution_convert_fusion.1 = bf16[512,3584]{1,0:T(8,128)(2,1)} fusion(bf16[512,2048]{1,0:T(8,128)(2,1)S(1)} %bitcast.47, bf16[2048,3584]{1,0:T(8,128)(2,1)} %param.7), kind=kOutput, calls=%fused_computation.4 | convolution fusion | flops 7518027776 | bytes 20447232 | tf_op jit(solution)/shard_map/dot_general | solution.py:19
  69.9 6.0 %pad_maximum_fusion = bf16[512,7168]{1,0:T(8,128)(2,1)} fusion(bf16[512,3584]{1,0:T(8,128)(2,1)S(1)} %convolution_convert_fusion, bf16[512,3584]{1,0:T(8,128)(2,1)} %convolution_convert_fusion.1), kind=kLoop, calls=%fused_computation.2 | loop fusion | flops 14680064 | bytes 14680064 | tf_op jit(solution)/shard_map/concatenate | solution.py:21
  75.9 0.0 all-reduce.2.cloned.1.call-update
  75.9 0.0 reduce-scatter.4.cloned.1.call-start
  76.0 137.9 %all-reduce.2.cloned.1.call-done = bf16[512,7168]{1,0:T(8,128)(2,1)} async-done(((bf16[512,7168]{1,0:T(8,128)(2,1)}), bf16[512,7168]{1,0:T(8,128)(2,1)}) %all-reduce.2.cloned.1.call-update) | async-done | bytes 7340048 | tf_op jit(solution)/shard_map/psum | solution.py:22
  213.9 10.2 %convert_element_type.29 = f32[512,7168]{1,0:T(8,128)} convert(bf16[512,7168]{1,0:T(8,128)(2,1)} %all-reduce.2.cloned.1.call-done) | non-fusion elementwise | flops 3670016 | bytes 22020096 | tf_op jit(solution)/shard_map/convert_element_type | solution.py:22
  224.1 0.0 copy-start.1
  224.1 16.5 %fusion.3 = bf16[512,2048]{1,0:T(8,128)(2,1)} fusion(bf16[3584,2048]{1,0:T(8,128)(2,1)} %param.9, f32[512,7168]{1,0:T(8,128)} %convert_element_type.29), kind=kOutput, calls=%fused_computation.6 | convolution fusion | flops 7528251392 | bytes 31457280 | tf_op jit(solution)/shard_map/dot_general | solution.py:25
  240.6 0.0 copy-start.2
  240.6 0.0 reduce-scatter.4.cloned.1.call-update
  240.6 0.0 copy-done.1
  240.6 22.3 %all_gather.6 = bf16[16,128,128]{2,1,0:T(8,128)(2,1)S(1)} all-gather(bf16[16,32,128]{2,1,0:T(8,128)(2,1)S(1)} %copy-done.1), channel_id=1, replica_groups=mesh['groups'=2,'fsdp'=4,'tensor'=4] {'tensor'}, dimensions={1}, use_global_device_ids=true | all-gather | bytes 655360 | tf_op jit(solution)/shard_map/all_gather | solution.py:31
  262.9 1.1 constant_dynamic-slice_fusion
  264.0 0.3 copy.29
  264.2 0.5 fusion.9
  264.8 1.2 copy.31
  266.0 3.5 all-to-all-start.1
  269.4 0.0 reduce-scatter.8.cloned.1.call-start
  269.5 0.0 copy-done.2
  269.5 22.2 %all_gather.7 = bf16[32,64,64]{2,1,0:T(8,128)(2,1)S(1)} all-gather(bf16[32,16,64]{2,1,0:T(8,128)(2,1)S(1)} %copy-done.2), channel_id=1, replica_groups=mesh['groups'=2,'fsdp'=4,'tensor'=4] {'tensor'}, dimensions={1}, use_global_device_ids=true | all-gather | bytes 327680 | tf_op jit(solution)/shard_map/all_gather | solution.py:32
  291.7 0.0 all-to-all-done.1
  291.7 0.1 copy.33
  291.7 6.0 %reduce-scatter.4.cloned.1.call-done = bf16[128,2048]{1,0:T(8,128)(2,1)} async-done(((bf16[512,2048]{1,0:T(8,128)(2,1)}), bf16[128,2048]{1,0:T(8,128)(2,1)}) %reduce-scatter.4.cloned.1.call-update) | async-done | bytes 524304 | tf_op jit(solution)/shard_map/reduce_scatter | solution.py:24
  297.7 1.2 copy.34
  299.0 0.3 fusion.7
  299.3 1.4 fusion.12
  300.7 0.0 reduce-scatter.8.cloned.1.call-update
  300.7 0.0 reduce-scatter.6.cloned.1.call-start
  300.8 0.3 fusion.8
  301.1 0.3 copy.35
  301.5 11.3 %all_to_all.56 = bf16[128,64,32]{0,2,1:T(8,128)(2,1)S(1)} all-to-all(bf16[128,64,32]{0,2,1:T(8,128)(2,1)S(1)} %copy.35), channel_id=1, replica_groups=mesh['groups'=2,'fsdp'=4,'tensor'=4] {'fsdp'}, dimensions={1} | all-to-all | bytes 1048576 | tf_op jit(solution)/shard_map/all_to_all | solution.py:48
  312.8 1.5 fusion.11
  314.3 0.0 reduce-scatter.6.cloned.1.call-update
  314.3 14.2 %reduce-scatter.8.cloned.1.call-done = f32[32,16,64]{2,1,0:T(8,128)} async-done(((f32[32,64,64]{2,1,0:T(8,128)}), f32[32,16,64]{2,1,0:T(8,128)}) %reduce-scatter.8.cloned.1.call-update) | async-done | bytes 131088 | tf_op jit(solution)/shard_map/reduce_scatter | solution.py:54
  328.5 28.5 %reduce-scatter.6.cloned.1.call-done = f32[16,32,128]{2,1,0:T(8,128)} async-done(((f32[16,128,128]{2,1,0:T(8,128)}), f32[16,32,128]{2,1,0:T(8,128)}) %reduce-scatter.6.cloned.1.call-update) | async-done | bytes 262160 | tf_op jit(solution)/shard_map/reduce_scatter | solution.py:53
  (1 shorter events, 0.0 us)
Async XLA Ops:
  7.2 206.7 %all-reduce.2.cloned.1.call-start = ((), (), s32[]{:S(2)}) async-start(), calls=%async_computation.6 | async-start | bytes 14680064 | tf_op jit(solution)/shard_map/psum | solution.py:22
  43.8 13.7 %copy-start = (bf16[4,128,2048]{2,1,0:T(8,128)(2,1)S(1)}, bf16[4,128,2048]{2,1,0:T(8,128)(2,1)}, u32[]{:S(2)}) copy-start(bf16[4,128,2048]{2,1,0:T(8,128)(2,1)} %copy.28) | copy-start | bytes 6291460
  75.9 221.8 %reduce-scatter.4.cloned.1.call-start = ((), (), s32[]{:S(2)}) async-start(), calls=%async_computation.7 | async-start | bytes 2621440 | tf_op jit(solution)/shard_map/reduce_scatter | solution.py:24
  224.1 16.6 %copy-start.1 = (bf16[16,32,128]{2,1,0:T(8,128)(2,1)S(1)}, bf16[16,32,128]{2,1,0:T(8,128)(2,1)}, u32[]{:S(2)}) copy-start(bf16[16,32,128]{2,1,0:T(8,128)(2,1)} %param.10) | copy-start | bytes 393220
  240.6 28.9 %copy-start.2 = (bf16[32,16,64]{2,1,0:T(8,128)(2,1)S(1)}, bf16[32,16,64]{2,1,0:T(8,128)(2,1)}, u32[]{:S(2)}) copy-start(bf16[32,16,64]{2,1,0:T(8,128)(2,1)} %param.11) | copy-start | bytes 196612
  266.0 25.7 %all-to-all-start.1 = ((bf16[128,16,128]{0,1,2:T(8,128)(2,1)}), bf16[128,16,128]{0,1,2:T(8,128)(2,1)S(1)}, u32[]{:S(2)}, u32[]{:S(2)}) async-start(bf16[128,16,128]{0,1,2:T(8,128)(2,1)} %copy.31), calls=%async_computation.1 | async-start | bytes 1048576 | tf_op jit(solution)/shard_map/all_to_all | solution.py:40
  269.4 59.0 %reduce-scatter.8.cloned.1.call-start = ((), (), s32[]{:S(2)}) async-start(), calls=%async_computation.9 | async-start | bytes 1310720 | tf_op jit(solution)/shard_map/reduce_scatter | solution.py:54
  300.7 56.3 %reduce-scatter.6.cloned.1.call-start = ((), (), s32[]{:S(2)}) async-start(), calls=%async_computation.8 | async-start | bytes 1310720 | tf_op jit(solution)/shard_map/reduce_scatter | solution.py:53
Sparse Core Ops, SparseCore 0:
  76.1 137.7 all-reduce.1
  240.7 56.9 reduce-scatter.3
  300.9 27.5 reduce-scatter.7
  331.2 25.7 reduce-scatter.5
where the time goes:
time: 364 us
  waiting for transfers between devices  187 us (51%)
  blocking collectives  85.6 us (24%)
  matrix products  46.6 us (13%)
  other arithmetic  16.2 us (4%)
  between operations  13.9 us (4%)
  local copies, waits for them, and re-layouts  11 us (3%)
  starting transfers between devices  3.64 us (1%)
    psum x1, waiting for transfers between devices, body(): lax.psum(partial_value.astype(jnp.bfloat16), 'fsdp').astype(jnp.float32)  138 us
    all_to_all x1, blocking collectives, body(): lax.all_to_all(tokens, 'fsdp', split_axis=1, concat_axis=0, tiled=True)  29.9 us
    reduce_scatter x1, waiting for transfers between devices, body(): lax.psum_scatter(grad_right, 'tensor', scatter_dimension=1, tiled=True)  28.5 us
    all_gather x1, blocking collectives, body(): lax.all_gather(right_factor, 'tensor', axis=1, tiled=True)  22.3 us
    all_gather x1, blocking collectives, body(): lax.all_gather(left_factor, 'tensor', axis=1, tiled=True)  22.2 us
    dot_general x1, matrix products, body(): jnp.dot(hidden, down_weight, preferred_element_type=jnp.float32)  16.5 us
    reduce_scatter x1, waiting for transfers between devices, body(): lax.psum_scatter(grad_left, 'tensor', scatter_dimension=1, tiled=True)  14.2 us
    dot_general x1, matrix products, body(): up_part = jnp.dot(spread, up_weight, preferred_element_type=jnp.float32)  13.7 us
  transfers between devices with their start and end apart: 5, of which 4 were waited for; matrix products, arithmetic and copies ran while one was open for 1% of the time, Pallas kernels for 0%

commit v1 on v0

--- a/solution.py
+++ b/solution.py
@@ -19,7 +19,9 @@
     gate_part = jnp.dot(spread, gate_weight, preferred_element_type=jnp.float32)
     up_part = jnp.dot(spread, up_weight, preferred_element_type=jnp.float32)
     partial_value = jnp.concatenate([gate_part, up_part], axis=1)
-    summed = lax.psum(partial_value.astype(jnp.bfloat16), "fsdp").astype(jnp.float32)
+    summed = jnp.sum(lax.all_gather(partial_value.astype(jnp.bfloat16), "fsdp"), axis=0).astype(
+        jnp.float32
+    )
     hidden = (jax.nn.silu(summed[:, :hid_local]) * summed[:, hid_local:]).astype(jnp.bfloat16)
     target = lax.psum_scatter(
         jnp.dot(hidden, down_weight, preferred_element_type=jnp.float32).astype(jnp.bfloat16),

time: 364 us -> 420 us (1.15)
  waiting for transfers between devices: 187 us -> 228 us
  other arithmetic: 16.2 us -> 30.7 us
    all_gather x0 -> x1, waiting for transfers between devices: none -> 179 us  [body(): lax.all_gather(partial_value.astype(jnp.bfloat16), 'fsdp')]
    psum x1 -> x0, waiting for transfers between devices: 138 us -> none  [body(): lax.psum(partial_value.astype(jnp.bfloat16), 'fsdp').astype(jnp.float32)]
    reduce_sum x0 -> x1, other arithmetic: none -> 14.9 us  [body(): jnp.sum(lax.all_gather(partial_value.astype(jnp.bfloat16), 'fsdp'), axis=0)]
where the time goes in v1:
time: 420 us; the launch traced here: 419 us
  waiting for transfers between devices  228 us (54%)
  blocking collectives  85.7 us (20%)
  matrix products  46.7 us (11%)
  other arithmetic  30.7 us (7%)
  between operations  13.9 us (3%)
  local copies, waits for them, and re-layouts  11 us (3%)
    all_gather x1, waiting for transfers between devices, body(): lax.all_gather(partial_value.astype(jnp.bfloat16), 'fsdp')  179 us
    all_to_all x1, blocking collectives, body(): lax.all_to_all(tokens, 'fsdp', split_axis=1, concat_axis=0, tiled=True)  29.9 us
    reduce_scatter x1, waiting for transfers between devices, body(): lax.psum_scatter(grad_right, 'tensor', scatter_dimension=1, tiled=True)  28.5 us
    all_gather x1, blocking collectives, body(): lax.all_gather(left_factor, 'tensor', axis=1, tiled=True)  22.4 us
    all_gather x1, blocking collectives, body(): lax.all_gather(right_factor, 'tensor', axis=1, tiled=True)  22.1 us
    dot_general x1, matrix products, body(): jnp.dot(hidden, down_weight, preferred_element_type=jnp.float32)  16.5 us
    reduce_sum x1, other arithmetic, body(): jnp.sum(lax.all_gather(partial_value.astype(jnp.bfloat16), 'fsdp'), axis=0)  14.9 us
    dot_general x1, matrix products, body(): gate_part = jnp.dot(spread, gate_weight, preferred_element_type=jnp.float32)  13.8 us
  transfers between devices with their start and end apart: 5, of which 4 were waited for; matrix products, arithmetic and copies ran while one was open for 1% of the time, Pallas kernels for 0%

profile of v1, /device:TPU:0, one launch (start us, length us, event | category | flops | bytes accessed | tf_op | source)
XLA Modules:
  0.0 419.3 jit_solution(1726771100546967650)
XLA Ops:
  7.2 0.0 all-gather.2.cloned.1.call-start
  7.2 4.1 copy.27
  11.3 29.9 %all_to_all.55 = bf16[128,4,2048]{0,2,1:T(8,128)(2,1)S(1)} all-to-all(bf16[128,4,2048]{0,2,1:T(8,128)(2,1)} %bitcast.43), channel_id=1, replica_groups=mesh['groups'=2,'fsdp'=4,'tensor'=4] {'fsdp'}, dimensions={1} | all-to-all | bytes 4194304 | tf_op jit(solution)/shard_map/all_to_all | solution.py:15
  41.2 2.6 copy.28
  43.8 0.0 copy-start
  43.8 13.8 %fusion.1 = bf16[1,512,3584]{2,1,0:T(8,128)(2,1)S(1)} fusion(bf16[512,2048]{1,0:T(8,128)(2,1)} %bitcast.49, bf16[2048,3584]{1,0:T(8,128)(2,1)} %param.7), kind=kOutput, calls=%fused_computation.5 | convolution fusion | flops 7518027776 | bytes 20447232 | tf_op jit(solution)/shard_map/dot_general | solution.py:19
  57.6 0.0 copy-done
  57.6 12.4 %fusion.2 = bf16[1,512,3584]{2,1,0:T(8,128)(2,1)} fusion(bf16[512,2048]{1,0:T(8,128)(2,1)S(1)} %bitcast.51, bf16[2048,3584]{1,0:T(8,128)(2,1)} %param.8), kind=kOutput, calls=%fused_computation.6 | convolution fusion | flops 7518027776 | bytes 20447232 | tf_op jit(solution)/shard_map/dot_general | solution.py:20
  70.0 5.7 %pad_maximum_fusion = bf16[1,512,7168]{2,1,0:T(8,128)(2,1)} fusion(bf16[1,512,3584]{2,1,0:T(8,128)(2,1)} %fusion.2, bf16[1,512,3584]{2,1,0:T(8,128)(2,1)S(1)} %fusion.1), kind=kLoop, calls=%fused_computation.2 | loop fusion | flops 14680064 | bytes 14680064 | tf_op jit(solution)/shard_map/concatenate | solution.py:21
  75.7 0.0 all-gather.2.cloned.1.call-update
  75.7 0.2 reduce-scatter.4.cloned.1.call-start
  75.9 179.1 %all-gather.2.cloned.1.call-done = bf16[4,512,7168]{2,1,0:T(8,128)(2,1)} async-done(((bf16[1,512,7168]{2,1,0:T(8,128)(2,1)}), bf16[4,512,7168]{2,1,0:T(8,128)(2,1)}) %all-gather.2.cloned.1.call-update) | async-done | bytes 29360144 | tf_op jit(solution)/shard_map/all_gather | solution.py:22
  255.0 14.9 %reduce_sum.12 = bf16[512,7168]{1,0:T(8,128)(2,1)} reduce(bf16[4,512,7168]{2,1,0:T(8,128)(2,1)} %all-gather.2.cloned.1.call-done, bf16[]{:T(256)} %constant.6.clone.1), dimensions={0}, to_apply=%region_0.0 | reduce | flops 11010048 | bytes 36700160 | tf_op jit(solution)/shard_map/reduce_sum | solution.py:22
  269.9 10.2 %convert_element_type.38 = f32[512,7168]{1,0:T(8,128)} convert(bf16[512,7168]{1,0:T(8,128)(2,1)} %reduce_sum.12) | non-fusion elementwise | flops 3670016 | bytes 22020096 | tf_op jit(solution)/shard_map/convert_element_type | solution.py:22
  280.1 0.0 copy-start.1
  280.1 16.5 %fusion.5 = bf16[512,2048]{1,0:T(8,128)(2,1)} fusion(bf16[3584,2048]{1,0:T(8,128)(2,1)} %param.9, f32[512,7168]{1,0:T(8,128)} %convert_element_type.38), kind=kOutput, calls=%fused_computation.8 | convolution fusion | flops 7528251392 | bytes 31457280 | tf_op jit(solution)/shard_map/dot_general | solution.py:27
  296.6 0.0 copy-start.2
  296.6 0.0 reduce-scatter.4.cloned.1.call-update
  296.6 0.0 copy-done.1
  296.6 22.1 %all_gather.10 = bf16[16,128,128]{2,1,0:T(8,128)(2,1)S(1)} all-gather(bf16[16,32,128]{2,1,0:T(8,128)(2,1)S(1)} %copy-done.1), channel_id=1, replica_groups=mesh['groups'=2,'fsdp'=4,'tensor'=4] {'tensor'}, dimensions={1}, use_global_device_ids=true | all-gather | bytes 655360 | tf_op jit(solution)/shard_map/all_gather | solution.py:33
  318.8 1.1 constant_dynamic-slice_fusion
  319.8 0.3 copy.29
  320.1 0.5 fusion.11
  320.6 1.2 copy.31
  321.8 3.5 all-to-all-start.1
  325.3 0.0 reduce-scatter.8.cloned.1.call-start
  325.4 0.0 copy-done.2
  325.4 22.4 %all_gather.11 = bf16[32,64,64]{2,1,0:T(8,128)(2,1)S(1)} all-gather(bf16[32,16,64]{2,1,0:T(8,128)(2,1)S(1)} %copy-done.2), channel_id=1, replica_groups=mesh['groups'=2,'fsdp'=4,'tensor'=4] {'tensor'}, dimensions={1}, use_global_device_ids=true | all-gather | bytes 327680 | tf_op jit(solution)/shard_map/all_gather | solution.py:34
  347.8 0.0 all-to-all-done.1
  347.8 0.1 copy.33
  347.9 6.3 %reduce-scatter.4.cloned.1.call-done = bf16[128,2048]{1,0:T(8,128)(2,1)} async-done(((bf16[512,2048]{1,0:T(8,128)(2,1)}), bf16[128,2048]{1,0:T(8,128)(2,1)}) %reduce-scatter.4.cloned.1.call-update) | async-done | bytes 524304 | tf_op jit(solution)/shard_map/reduce_scatter | solution.py:26
  354.2 1.2 copy.34
  355.5 0.3 fusion.9
  355.7 1.4 fusion.14
  357.2 0.0 reduce-scatter.8.cloned.1.call-update
  357.2 0.0 reduce-scatter.6.cloned.1.call-start
  357.2 0.3 fusion.10
  357.6 0.3 copy.35
  357.9 11.2 %all_to_all.56 = bf16[128,64,32]{0,2,1:T(8,128)(2,1)S(1)} all-to-all(bf16[128,64,32]{0,2,1:T(8,128)(2,1)S(1)} %copy.35), channel_id=1, replica_groups=mesh['groups'=2,'fsdp'=4,'tensor'=4] {'fsdp'}, dimensions={1} | all-to-all | bytes 1048576 | tf_op jit(solution)/shard_map/all_to_all | solution.py:50
  369.2 1.5 fusion.13
  370.7 0.0 reduce-scatter.6.cloned.1.call-update
  370.7 13.5 %reduce-scatter.8.cloned.1.call-done = f32[32,16,64]{2,1,0:T(8,128)} async-done(((f32[32,64,64]{2,1,0:T(8,128)}), f32[32,16,64]{2,1,0:T(8,128)}) %reduce-scatter.8.cloned.1.call-update) | async-done | bytes 131088 | tf_op jit(solution)/shard_map/reduce_scatter | solution.py:56
  384.3 28.5 %reduce-scatter.6.cloned.1.call-done = f32[16,32,128]{2,1,0:T(8,128)} async-done(((f32[16,128,128]{2,1,0:T(8,128)}), f32[16,32,128]{2,1,0:T(8,128)}) %reduce-scatter.6.cloned.1.call-update) | async-done | bytes 262160 | tf_op jit(solution)/shard_map/reduce_scatter | solution.py:55
  (1 shorter events, 0.0 us)
Async XLA Ops:
  7.2 247.9 %all-gather.2.cloned.1.call-start = ((), (), s32[]{:S(2)}) async-start(), calls=%async_computation.6 | async-start | bytes 36700160 | tf_op jit(solution)/shard_map/all_gather | solution.py:22
  43.8 13.8 %copy-start = (bf16[4,128,2048]{2,1,0:T(8,128)(2,1)S(1)}, bf16[4,128,2048]{2,1,0:T(8,128)(2,1)}, u32[]{:S(2)}) copy-start(bf16[4,128,2048]{2,1,0:T(8,128)(2,1)} %copy.28) | copy-start | bytes 6291460
  75.7 278.5 %reduce-scatter.4.cloned.1.call-start = ((), (), s32[]{:S(2)}) async-start(), calls=%async_computation.7 | async-start | bytes 2621440 | tf_op jit(solution)/shard_map/reduce_scatter | solution.py:26
  280.1 16.6 %copy-start.1 = (bf16[16,32,128]{2,1,0:T(8,128)(2,1)S(1)}, bf16[16,32,128]{2,1,0:T(8,128)(2,1)}, u32[]{:S(2)}) copy-start(bf16[16,32,128]{2,1,0:T(8,128)(2,1)} %param.10) | copy-start | bytes 393220
  296.6 28.8 %copy-start.2 = (bf16[32,16,64]{2,1,0:T(8,128)(2,1)S(1)}, bf16[32,16,64]{2,1,0:T(8,128)(2,1)}, u32[]{:S(2)}) copy-start(bf16[32,16,64]{2,1,0:T(8,128)(2,1)} %param.11) | copy-start | bytes 196612
  321.8 26.0 %all-to-all-start.1 = ((bf16[128,16,128]{0,1,2:T(8,128)(2,1)}), bf16[128,16,128]{0,1,2:T(8,128)(2,1)S(1)}, u32[]{:S(2)}, u32[]{:S(2)}) async-start(bf16[128,16,128]{0,1,2:T(8,128)(2,1)} %copy.31), calls=%async_computation.1 | async-start | bytes 1048576 | tf_op jit(solution)/shard_map/all_to_all | solution.py:42
  325.3 59.0 %reduce-scatter.8.cloned.1.call-start = ((), (), s32[]{:S(2)}) async-start(), calls=%async_computation.9 | async-start | bytes 1310720 | tf_op jit(solution)/shard_map/reduce_scatter | solution.py:56
  357.2 55.6 %reduce-scatter.6.cloned.1.call-start = ((), (), s32[]{:S(2)}) async-start(), calls=%async_computation.8 | async-start | bytes 1310720 | tf_op jit(solution)/shard_map/reduce_scatter | solution.py:55
Sparse Core Ops, SparseCore 0:
  75.8 179.1 all-gather.1
  296.7 57.4 reduce-scatter.3
  357.3 26.8 reduce-scatter.7
  387.0 25.7 reduce-scatter.5
